TPU v7x, 32 devices: a whole 2x2x4 slice. The times are simulated.
32 devices in a mesh: groups: 2 (over y), sect: 4 (over x, core), hid: 4 (over z).
Axes of the slice: x: 2, y: 2, z: 4, core: 2. Of those that a mesh axis runs over, the one named last changes fastest.
Arguments:
- resid: bfloat16 [1024, 4096], P(('groups', 'sect'), 'hid'), parts along dimension 0, may hold values from -64 to 64
- moe_gain: bfloat16 [4096], replicated, may hold values from 0.25 to 1.75
- routes: int32 [1024, 2], P(('groups', 'sect')), parts along dimension 0, may hold values from 0 to 3, all different within a row; in each aligned block of 128 rows (0 to 127, 128 to 255, ...) at most 128 rows name the same one
- gate_q: int32 [1024, 2], P(('groups', 'sect')), parts along dimension 0, may hold values from 16 to 255
- doc_lengths: int32 [8, 4], P(('groups', 'sect')), parts along dimension 0, may hold values from 1 to 64, 128 in all within a row
- w_gate: bfloat16 [4, 4096, 4096], P('sect', None, 'hid'), may hold values from -0.09375 to 0.09375
- w_up: bfloat16 [4, 4096, 4096], P('sect', None, 'hid'), may hold values from -0.09375 to 0.09375
- w_down: bfloat16 [4, 4096, 4096], P('sect', 'hid'), may hold values from -0.09375 to 0.09375
- attn_gain: bfloat16 [4096], replicated, may hold values from 0.25 to 1.75
- w_q: bfloat16 [4096, 4096], P('sect', 'hid')
- w_k: bfloat16 [4096, 1024], P('sect', 'hid')
- w_v: bfloat16 [4096, 1024], P('sect', 'hid'), may hold values from -0.09375 to 0.09375
Outputs:
- new_resid: bfloat16 [1024, 4096], P(('groups', 'sect'), 'hid'), parts along dimension 0
- context: bfloat16 [1024, 4096], P(('groups', 'sect'), 'hid'), parts along dimension 0
There are 2 independent parts, one for each index of `groups`. A program takes and returns all parts, laid end to end along the dimension named above; an argument that names none is the same for every part. Nothing has to cross between parts.
Inputs may be any that keep to these rules, and one draw needn't show every extreme that they name: `routes`: within the rows of one index of sect (aligned blocks of 128 rows) no expert is named by more than 128 rows. `doc_lengths`: each row sums to 128.
All inputs are finite; a program needn't handle non-finite values.
Results may differ from a plain program's by a relative error of at most 0.012.
The roundings to bfloat16 on the way count: a program that leaves them out, or rounds other values in their place, can miss the bound.
Values may be sent and summed in bfloat16 or wider, within the bound.
No kernel may reach another device: no remote copies, remote signals or barrier semaphores. Data moves between devices by JAX's collectives and lax.ppermute only.
A program may use at most 128 MiB of HBM per device.

v0:
```python
import math
import jax
import jax.numpy as jnp
from jax import lax
from jax.sharding import PartitionSpec as P

H = 32
KVH = 8
HD = 128


def layer_norm(values, gain):
    center = values - jnp.mean(values, axis=1, keepdims=True)
    spread = jnp.mean(center * center, axis=1, keepdims=True)
    return (center * lax.rsqrt(spread + 1e-05) * gain.astype(jnp.float32)).astype(jnp.bfloat16)


def slot_targets(route_rows, experts, capacity):
    flat = route_rows.reshape(-1)
    onehot = (flat[:, None] == jnp.arange(experts, dtype=jnp.int32)[None, :]).astype(jnp.int32)
    before = jnp.cumsum(onehot, axis=0, dtype=jnp.int32) - onehot
    return flat * capacity + jnp.sum(before * onehot, axis=1, dtype=jnp.int32)


def source_rows(targets, experts, capacity):
    count = targets.shape[0]
    filler = jnp.full((experts * capacity,), count, jnp.int32)
    return filler.at[targets].set(jnp.arange(count, dtype=jnp.int32)) // 2


def rotate(values, position, head):
    count = values.shape[0]
    split_heads = values.reshape(count, -1, head)
    half = head // 2
    freqs = jnp.exp(jnp.arange(half, dtype=jnp.float32) * (-2.0 * math.log(10000.0) / head))
    angles = position[:, None, None] * freqs[None, None, :]
    cosine = jnp.cos(angles)
    sine = jnp.sin(angles)
    first = split_heads[:, :, :half]
    second = split_heads[:, :, half:]
    turned = jnp.concatenate(
        [first * cosine - second * sine, second * cosine + first * sine], axis=2
    )
    return turned.reshape(count, -1)


def attend(query, keys, vals, lengths, head, group):
    count = query.shape[0]
    kv_heads = keys.shape[1] // head
    ends = jnp.cumsum(lengths, dtype=jnp.int32)
    places = jnp.arange(count, dtype=jnp.int32)
    after = (places[:, None] >= ends[None, :]).astype(jnp.int32)
    doc_ids = jnp.sum(after, axis=1, dtype=jnp.int32)
    starts = jnp.sum(after * lengths[None, :], axis=1, dtype=jnp.int32)
    position = (places - starts).astype(jnp.float32)
    rotated_q = (
        rotate(query, position, head).astype(jnp.bfloat16).reshape(count, kv_heads, group, head)
    )
    rotated_k = rotate(keys, position, head).astype(jnp.bfloat16).reshape(count, kv_heads, head)
    value_heads = vals.reshape(count, kv_heads, head)
    allowed = (doc_ids[:, None] == doc_ids[None, :]) & (places[None, :] <= places[:, None])
    scores = jnp.einsum(
        "tkgd,skd->kgts", rotated_q, rotated_k, preferred_element_type=jnp.float32
    ) * (1.0 / math.sqrt(head))
    scores = jnp.where(allowed[None, None], scores, -jnp.inf)
    highest = jnp.max(scores, axis=3, keepdims=True)
    weights = jnp.exp(scores - highest)
    probs = (weights / jnp.sum(weights, axis=3, keepdims=True)).astype(jnp.bfloat16)
    mixed = jnp.einsum("kgts,skd->tkgd", probs, value_heads, preferred_element_type=jnp.float32)
    return mixed.astype(jnp.bfloat16).reshape(count, -1)


def on_device(
    resid, moe_gain, routes, gate_q, doc_lengths, w_gate, w_up, w_down, attn_gain, w_q, w_k, w_v
):
    sections = lax.axis_size("sect")
    slices = lax.axis_size("hid")
    tokens_here, local_width = resid.shape
    width = local_width * slices
    capacity = 4 * tokens_here // sections
    entry = lax.all_gather(resid, "hid", axis=1, tiled=True)
    normed = layer_norm(entry.astype(jnp.float32), moe_gain)
    targets = slot_targets(routes, sections, capacity)
    sources = source_rows(targets, sections, capacity)
    padded = jnp.concatenate([normed, jnp.zeros((1, width), jnp.bfloat16)], axis=0)
    gate_w = w_gate[0]
    up_w = w_up[0]
    down_w = w_down[0]
    outgoing = padded[sources].reshape(sections, capacity, width)
    arrived = lax.all_to_all(outgoing, "sect", split_axis=0, concat_axis=0, tiled=True).reshape(
        sections * capacity, width
    )
    gate = jnp.dot(arrived, gate_w, preferred_element_type=jnp.float32)
    up = jnp.dot(arrived, up_w, preferred_element_type=jnp.float32)
    hidden = (jax.nn.silu(gate) * up).astype(jnp.bfloat16)
    weights = gate_q.reshape(-1).astype(jnp.float32) / 256.0
    own_resid = resid.astype(jnp.float32)
    outputs = jnp.dot(hidden, down_w, preferred_element_type=jnp.float32)
    mine = lax.psum_scatter(outputs, "hid", scatter_dimension=1, tiled=True)
    returned = lax.all_to_all(
        mine.reshape(sections, capacity, local_width),
        "sect",
        split_axis=0,
        concat_axis=0,
        tiled=True,
    )
    picked = returned.reshape(sections * capacity, local_width)[targets]
    mixture = jnp.sum((picked * weights[:, None]).reshape(tokens_here, 2, local_width), axis=1)
    new_local = (own_resid + mixture).astype(jnp.bfloat16)
    full_rows = lax.all_gather(new_local, "hid", axis=1, tiled=True)
    normed_next = layer_norm(full_rows.astype(jnp.float32), attn_gain)
    query = jnp.dot(
        normed_next,
        lax.all_gather(w_q, "sect", axis=0, tiled=True),
        preferred_element_type=jnp.float32,
    )
    keys = jnp.dot(
        normed_next,
        lax.all_gather(w_k, "sect", axis=0, tiled=True),
        preferred_element_type=jnp.float32,
    )
    vals = jnp.dot(
        normed_next,
        lax.all_gather(w_v, "sect", axis=0, tiled=True),
        preferred_element_type=jnp.float32,
    )
    context = attend(query, keys, vals.astype(jnp.bfloat16), doc_lengths[0], HD, H // KVH)
    return (new_local, context)


def solution(mesh):
    in_specs = (
        P(("groups", "sect"), "hid"),
        P(),
        P(("groups", "sect"), None),
        P(("groups", "sect"), None),
        P(("groups", "sect"), None),
        P("sect", None, "hid"),
        P("sect", None, "hid"),
        P("sect", "hid", None),
        P(),
        P("sect", "hid"),
        P("sect", "hid"),
        P("sect", "hid"),
    )
    out_specs = (P(("groups", "sect"), "hid"), P(("groups", "sect"), "hid"))
    return jax.shard_map(
        on_device, mesh=mesh, in_specs=in_specs, out_specs=out_specs, check_vma=False
    )
```

profile of v0, /device:TPU:0, one launch (start us, length us, event | category | flops | bytes accessed | tf_op | source)
XLA Modules:
  0.0 450.2 jit_solution(11100007344031387848)
XLA Ops:
  7.2 0.7 all-gather.6.cloned.1.call-update
  7.9 0.8 copy.36
  9.0 0.7 convert_element_type.72
  9.7 1.2 reduce-window.18
  11.2 0.7 broadcast_multiply_fusion
  12.3 1.4 scatter_custom_fusion
  13.7 26.5 %all-gather.6.cloned.1.call-done = bf16[128,4096]{1,0:T(8,128)(2,1)} async-done(((bf16[128,1024]{1,0:T(8,128)(2,1)}), bf16[128,4096]{1,0:T(8,128)(2,1)}) %all-gather.6.cloned.1.call-update) | async-done | bytes 1048592 | tf_op jit(solution)/shard_map/all_gather | solution.py:81
  40.2 1.5 convert_reduce_fusion.1
  41.8 1.7 fusion.14
  44.0 4.4 gather_fusion
  48.3 51.9 %all_to_all.10 = bf16[4,128,4096]{2,1,0:T(8,128)(2,1)S(1)} all-to-all(bf16[4,128,4096]{2,1,0:T(8,128)(2,1)} %bitcast.87), channel_id=1, replica_groups=mesh['groups'=2,'sect'=4,'hid'=4] {'sect'}, dimensions={0} | all-to-all | bytes 8388608 | tf_op jit(solution)/shard_map/all_to_all | solution.py:90
  100.2 2.0 copy-done.1
  102.2 6.9 %fusion.5 = f32[512,1024]{1,0:T(8,128)S(1)} fusion(bf16[512,4096]{1,0:T(8,128)(2,1)S(1)} %bitcast.89, bf16[1,4096,1024]{2,1,0:T(8,128)(2,1)} %param.17), kind=kOutput, calls=%fused_computation.8 | convolution fusion | flops 4294967296 | bytes 14680064 | tf_op jit(solution)/shard_map/dot_general | solution.py:93
  109.1 19.1 %fusion.1 = f32[512,4096]{1,0:T(8,128)} fusion(bf16[1,1024,4096]{2,1,0:T(8,128)(2,1)} %param.19, f32[512,1024]{1,0:T(8,128)S(1)} %fusion.5, bf16[512,4096]{1,0:T(8,128)(2,1)} %bitcast.90, bf16[1,4096,1024]{2,1,0:T(8,128)(2,1)} %param.18), kind=kOutput, calls=%fused_computation.4 | convolution fusion | flops 8593080320 | bytes 31457280 | tf_op jit(solution)/shard_map/dot_general | solution.py:98
  128.2 143.2 %reduce-scatter.2.cloned.1.call-done = f32[512,1024]{1,0:T(8,128)} async-done(((f32[512,4096]{1,0:T(8,128)}), f32[512,1024]{1,0:T(8,128)}) %reduce-scatter.2.cloned.1.call-update) | async-done | bytes 2097168 | tf_op jit(solution)/shard_map/reduce_scatter | solution.py:99
  271.4 3.7 all-to-all-start.1
  275.5 25.3 %all-to-all-done.1 = f32[4,128,1024]{2,1,0:T(8,128)S(1)} async-done(((f32[4,128,1024]{2,1,0:T(8,128)}), f32[4,128,1024]{2,1,0:T(8,128)S(1)}, u32[]{:S(2)}, u32[]{:S(2)}) %all-to-all-start.1) | async-done | bytes 2097184 | tf_op jit(solution)/shard_map/all_to_all | solution.py:100
  300.8 1.1 gather_fusion.1
  301.9 0.6 gather.10
  302.6 1.3 multiply_reduce_fusion
  303.9 0.8 add_convert_fusion.1
  305.4 0.5 all-gather.14.cloned.1.call-update
  307.2 25.4 %all-gather.8.cloned.1.call-done = bf16[128,4096]{1,0:T(8,128)(2,1)} async-done(((bf16[128,1024]{1,0:T(8,128)(2,1)}), bf16[128,4096]{1,0:T(8,128)(2,1)}) %all-gather.8.cloned.1.call-update) | async-done | bytes 1048592 | tf_op jit(solution)/shard_map/all_gather | solution.py:110
  332.6 1.5 convert_reduce_fusion
  334.2 1.7 fusion.11
  335.9 20.3 %all-gather.12.cloned.1.call-done = bf16[4096,256]{1,0:T(8,128)(2,1)} async-done(((bf16[1024,256]{1,0:T(8,128)(2,1)}), bf16[4096,256]{1,0:T(8,128)(2,1)}) %all-gather.12.cloned.1.call-update) | async-done | bytes 2097168 | tf_op jit(solution)/shard_map/all_gather | solution.py:119
  356.2 2.1 fusion.40
  358.4 57.5 %all-gather.14.cloned.1.call-done = bf16[4096,1024]{1,0:T(8,128)(2,1)} async-done(((bf16[1024,1024]{1,0:T(8,128)(2,1)}), bf16[4096,1024]{1,0:T(8,128)(2,1)}) %all-gather.14.cloned.1.call-update) | async-done | bytes 8388624 | tf_op jit(solution)/shard_map/all_gather | solution.py:114
  415.9 4.7 %convolution_bitcast_fusion = f32[16,8,8,128]{3,1,2,0:T(8,128)S(1)} fusion(bf16[4096,1024]{1,0:T(8,128)(2,1)} %all-gather.14.cloned.1.call-done, bf16[128,4096]{1,0:T(8,128)(2,1)S(1)} %copy-done.2, f32[4096]{0:T(1024)S(1)} %convert_element_type.80, f32[128]{0:T(128)S(1)} %add_rsqrt_fusion, f32[128]{0:T(128)S(1)} %broadcast_multiply_fusion.1), kind=kOutput, calls=%fused_computation.27 | convolution fusion | flops 1076363264 | bytes 9978880 | tf_op jit(solution)/shard_map/dot_general | solution.py:112
  422.1 17.9 %all-gather.10.cloned.1.call-done = bf16[4096,256]{1,0:T(8,128)(2,1)} async-done(((bf16[1024,256]{1,0:T(8,128)(2,1)}), bf16[4096,256]{1,0:T(8,128)(2,1)}) %all-gather.10.cloned.1.call-update) | async-done | bytes 2097168 | tf_op jit(solution)/shard_map/all_gather | solution.py:124
  439.9 2.1 convolution_convert_fusion.1
  442.5 0.9 copy.46
  (66 shorter events, 5.8 us)
Async XLA Ops:
  7.2 33.1 %all-gather.6.cloned.1.call-start = ((), (), s32[]{:S(2)}) async-start(), calls=%async_computation.3 | async-start | bytes 1310720 | tf_op jit(solution)/shard_map/all_gather | solution.py:81
  7.9 263.5 %reduce-scatter.2.cloned.1.call-start = ((), (), s32[]{:S(2)}) async-start(), calls=%async_computation.4 | async-start | bytes 10485760 | tf_op jit(solution)/shard_map/reduce_scatter | solution.py:99
  40.2 3.2 copy-start
  100.2 2.0 copy-start.1
  271.4 4.0 copy-start.5
  271.4 29.4 %all-to-all-start.1 = ((f32[4,128,1024]{2,1,0:T(8,128)}), f32[4,128,1024]{2,1,0:T(8,128)S(1)}, u32[]{:S(2)}, u32[]{:S(2)}) async-start(f32[4,128,1024]{2,1,0:T(8,128)} %bitcast.91), calls=%async_computation.2 | async-start | bytes 4194304 | tf_op jit(solution)/shard_map/all_to_all | solution.py:100
  275.2 57.5 %all-gather.8.cloned.1.call-start = ((), (), s32[]{:S(2)}) async-start(), calls=%async_computation.5 | async-start | bytes 1310720 | tf_op jit(solution)/shard_map/all_gather | solution.py:110
  301.9 2.0 copy-start.3
  303.9 2.6 copy-start.4
  303.9 2.6 copy-start.6
  304.7 51.4 %all-gather.12.cloned.1.call-start = ((), (), s32[]{:S(2)}) async-start(), calls=%async_computation.7 | async-start | bytes 2621440 | tf_op jit(solution)/shard_map/all_gather | solution.py:119
  305.3 110.6 %all-gather.14.cloned.1.call-start = ((), (), s32[]{:S(2)}) async-start(), calls=%async_computation.8 | async-start | bytes 10485760 | tf_op jit(solution)/shard_map/all_gather | solution.py:114
  305.9 134.0 %all-gather.10.cloned.1.call-start = ((), (), s32[]{:S(2)}) async-start(), calls=%async_computation.6 | async-start | bytes 2621440 | tf_op jit(solution)/shard_map/all_gather | solution.py:124
  332.6 23.5 %copy-start.2 = (bf16[128,4096]{1,0:T(8,128)(2,1)S(1)}, bf16[128,4096]{1,0:T(8,128)(2,1)}, u32[]{:S(2)}) copy-start(bf16[128,4096]{1,0:T(8,128)(2,1)} %all-gather.8.cloned.1.call-done) | copy-start | bytes 3145732
Sparse Core Ops, SparseCore 0:
  9.6 30.6 all-gather.5
  128.3 143.0 reduce-scatter.1
  304.9 27.7 all-gather.7
  334.1 22.0 all-gather.11
  357.6 58.2 all-gather.13
  417.3 22.5 all-gather.9
where the time goes:
time: 451 us; the launch traced here: 450 us
  waiting for transfers between devices  318 us (71%)
  blocking collectives  51.9 us (12%)
  matrix products  35.8 us (8%)
  between operations  14.4 us (3%)
  other arithmetic  12.8 us (3%)
  local copies, waits for them, and re-layouts  12.6 us (3%)
    reduce_scatter x1, waiting for transfers between devices, on_device(): mine = lax.psum_scatter(outputs, 'hid', scatter_dimension=1, tiled=True)  143 us
    all_gather x1, waiting for transfers between devices, on_device(): lax.all_gather(w_q, 'sect', axis=0, tiled=True)  57.5 us
    all_to_all x1, blocking collectives, on_device(): lax.all_to_all(outgoing, 'sect', split_axis=0, concat_axis=0, tiled=True)  51.9 us
    all_gather x1, waiting for transfers between devices, on_device(): entry = lax.all_gather(resid, 'hid', axis=1, tiled=True)  26.5 us
    all_gather x1, waiting for transfers between devices, on_device(): full_rows = lax.all_gather(new_local, 'hid', axis=1, tiled=True)  25.4 us
    all_to_all x1, waiting for transfers between devices, on_device(): lax.all_to_all(mine.reshape(sections, capacity, local_width), 'sect', spl...  25.3 us
    all_gather x1, waiting for transfers between devices, on_device(): lax.all_gather(w_k, 'sect', axis=0, tiled=True)  20.3 us
    dot_general x1, matrix products, on_device(): outputs = jnp.dot(hidden, down_w, preferred_element_type=jnp.float32)  19.1 us
  transfers between devices with their start and end apart: 7, of which 7 were waited for; matrix products, arithmetic and copies ran while one was open for 4% of the time, Pallas kernels for 0%

commit v1 on v0

--- a/solution.py
+++ b/solution.py
@@ -1,12 +1,43 @@
+import functools
 import math
 import jax
 import jax.numpy as jnp
 from jax import lax
 from jax.sharding import PartitionSpec as P
+from jax.lax import axis_index, axis_size, ppermute
 
 H = 32
 KVH = 8
 HD = 128
+
+
+def find_the_hubs(piece_in, at_axis, mesh_ax):
+    extent = axis_size(mesh_ax)
+    slots = []
+    dev_j = 0
+    while dev_j < extent:
+        slots.append((dev_j, (dev_j + 1) % extent))
+        dev_j = dev_j + 1
+    buffer = []
+    dev_j = 0
+    while dev_j < extent:
+        buffer.append((dev_j, (dev_j - 1) % extent))
+        dev_j += 1
+    r2, finding = ([piece_in], [piece_in])
+    for _ in range(extent // 2):
+        d_next = ppermute(r2[-1], mesh_ax, slots)
+        r2.append(d_next)
+    nth = 0
+    while nth < (extent - 1) // 2:
+        parts_out = ppermute(finding[-1], mesh_ax, buffer)
+        finding.append(parts_out)
+        nth += 1
+    wide_out = jnp.concatenate([*r2[::-1], *finding[1:]], axis=at_axis)
+    placed = axis_index(mesh_ax)
+    return jnp.roll(wide_out, (placed - extent // 2) * piece_in.shape[at_axis], axis=at_axis)
+
+
+arrange_tiles_over_axis = functools.partial(find_the_hubs, at_axis=1, mesh_ax="hid")
 
 
 def layer_norm(values, gain):
@@ -107,7 +138,7 @@
     picked = returned.reshape(sections * capacity, local_width)[targets]
     mixture = jnp.sum((picked * weights[:, None]).reshape(tokens_here, 2, local_width), axis=1)
     new_local = (own_resid + mixture).astype(jnp.bfloat16)
-    full_rows = lax.all_gather(new_local, "hid", axis=1, tiled=True)
+    full_rows = arrange_tiles_over_axis(new_local)
     normed_next = layer_norm(full_rows.astype(jnp.float32), attn_gain)
     query = jnp.dot(
         normed_next,

time: 451 us -> 360 us (0.80)
  waiting for transfers between devices: 318 us -> 224 us
  starting transfers between devices: 4.15 us -> 9.19 us
    all_gather x1, waiting for transfers between devices: 57.5 us -> 0.03 us  [on_device(): lax.all_gather(w_q, 'sect', axis=0, tiled=True)]
    all_gather x1 -> x0, waiting for transfers between devices: 25.4 us -> none  [on_device(): full_rows = lax.all_gather(new_local, 'hid', axis=1, tiled=True)]
    all_gather x1, waiting for transfers between devices: 20.3 us -> 0.03 us  [on_device(): lax.all_gather(w_k, 'sect', axis=0, tiled=True)]
    all_gather x1, waiting for transfers between devices: 17.9 us -> 0.03 us  [on_device(): lax.all_gather(w_v, 'sect', axis=0, tiled=True)]
    ppermute x0 -> x3, waiting for transfers between devices: none -> 17.1 us  [the longest x2 15.2 us: find_the_hubs(): d_next = ppermute(r2[-1], mesh_ax, slots)]
    all_to_all x1, waiting for transfers between devices: 25.3 us -> 35.9 us  [on_device(): lax.all_to_all(mine.reshape(sections, capacity, local_width), 'sect', spl...]
    ppermute x0 -> x3, starting transfers between devices: none -> 5.07 us  [the longest x1 3.84 us: find_the_hubs(): parts_out = ppermute(finding[-1], mesh_ax, buffer)]
  transfers between devices with their start and end apart: 7 -> 9, of which waited for: 7 -> 6; matrix products, arithmetic and copies ran while one was open for 4% -> 5% of each run, Pallas kernels for 0% -> 0%
where the time goes in v1:
time: 360 us; the launch traced here: 359 us
  waiting for transfers between devices  224 us (62%)
  blocking collectives  51.9 us (14%)
  matrix products  35.8 us (10%)
  between operations  16.1 us (4%)
  local copies, waits for them, and re-layouts  12.7 us (4%)
  other arithmetic  9.59 us (3%)
  starting transfers between devices  9.19 us (3%)
    reduce_scatter x1, waiting for transfers between devices, on_device(): mine = lax.psum_scatter(outputs, 'hid', scatter_dimension=1, tiled=True)  142 us
    all_to_all x1, blocking collectives, on_device(): lax.all_to_all(outgoing, 'sect', split_axis=0, concat_axis=0, tiled=True)  51.9 us
    all_to_all x1, waiting for transfers between devices, on_device(): lax.all_to_all(mine.reshape(sections, capacity, local_width), 'sect', spl...  35.9 us
    all_gather x1, waiting for transfers between devices, on_device(): entry = lax.all_gather(resid, 'hid', axis=1, tiled=True)  26.5 us
    dot_general x1, matrix products, on_device(): outputs = jnp.dot(hidden, down_w, preferred_element_type=jnp.float32)  19.1 us
    ppermute x2, waiting for transfers between devices, find_the_hubs(): d_next = ppermute(r2[-1], mesh_ax, slots)  15.2 us
  transfers between devices with their start and end apart: 9, of which 6 were waited for; matrix products, arithmetic and copies ran while one was open for 5% of the time, Pallas kernels for 0%

profile of v1, /device:TPU:0, one launch (start us, length us, event | category | flops | bytes accessed | tf_op | source)
XLA Modules:
  0.0 359.0 jit_solution(14182774999484378171)
XLA Ops:
  8.0 0.7 all-gather.5.cloned.1.call-update
  8.8 0.8 copy.36
  9.8 0.7 convert_element_type.72
  10.6 1.2 reduce-window.18
  12.1 0.7 broadcast_multiply_fusion
  13.1 1.4 scatter_custom_fusion
  14.6 26.5 %all-gather.5.cloned.1.call-done = bf16[128,4096]{1,0:T(8,128)(2,1)} async-done(((bf16[128,1024]{1,0:T(8,128)(2,1)}), bf16[128,4096]{1,0:T(8,128)(2,1)}) %all-gather.5.cloned.1.call-update) | async-done | bytes 1048592 | tf_op jit(solution)/shard_map/all_gather | solution.py:112
  41.1 1.5 convert_reduce_fusion.1
  42.6 1.7 fusion.14
  44.8 4.4 %gather_fusion = bf16[512,4096]{1,0:T(8,128)(2,1)} fusion(bf16[129,4096]{1,0:T(8,128)(2,1)S(1)} %concatenate.17, s32[1024]{0:T(1024)S(1)} %pad_clamp_fusion.1), kind=kCustom, calls=%fused_computation | custom fusion | bytes 8390656 | tf_op jit(solution)/shard_map/gather | solution.py:120
  49.2 51.9 %all_to_all.10 = bf16[4,128,4096]{2,1,0:T(8,128)(2,1)S(1)} all-to-all(bf16[4,128,4096]{2,1,0:T(8,128)(2,1)} %bitcast.87), channel_id=1, replica_groups=mesh['groups'=2,'sect'=4,'hid'=4] {'sect'}, dimensions={0} | all-to-all | bytes 8388608 | tf_op jit(solution)/shard_map/all_to_all | solution.py:121
  101.1 1.9 copy-done.1
  103.0 6.9 %fusion.5 = f32[512,1024]{1,0:T(8,128)S(1)} fusion(bf16[512,4096]{1,0:T(8,128)(2,1)S(1)} %bitcast.89, bf16[1,4096,1024]{2,1,0:T(8,128)(2,1)} %param.17), kind=kOutput, calls=%fused_computation.8 | convolution fusion | flops 4294967296 | bytes 14680064 | tf_op jit(solution)/shard_map/dot_general | solution.py:124
  109.9 19.1 %fusion.1 = f32[512,4096]{1,0:T(8,128)} fusion(bf16[1,1024,4096]{2,1,0:T(8,128)(2,1)} %param.19, f32[512,1024]{1,0:T(8,128)S(1)} %fusion.5, bf16[512,4096]{1,0:T(8,128)(2,1)} %bitcast.90, bf16[1,4096,1024]{2,1,0:T(8,128)(2,1)} %param.18), kind=kOutput, calls=%fused_computation.4 | convolution fusion | flops 8593080320 | bytes 31457280 | tf_op jit(solution)/shard_map/dot_general | solution.py:129
  129.0 0.5 all-gather.9.cloned.1.call-update
  129.6 0.5 all-gather.11.cloned.1.call-update
  130.1 142.1 %reduce-scatter.2.cloned.1.call-done = f32[512,1024]{1,0:T(8,128)} async-done(((f32[512,4096]{1,0:T(8,128)}), f32[512,1024]{1,0:T(8,128)}) %reduce-scatter.2.cloned.1.call-update) | async-done | bytes 2097168 | tf_op jit(solution)/shard_map/reduce_scatter | solution.py:130
  272.2 3.7 %all-to-all-start.1 = ((f32[4,128,1024]{2,1,0:T(8,128)}), f32[4,128,1024]{2,1,0:T(8,128)S(1)}, u32[]{:S(2)}, u32[]{:S(2)}) async-start(f32[4,128,1024]{2,1,0:T(8,128)} %bitcast.91), calls=%async_computation.2 | async-start | bytes 4194304 | tf_op jit(solution)/shard_map/all_to_all | solution.py:131
  276.9 35.9 %all-to-all-done.1 = f32[4,128,1024]{2,1,0:T(8,128)S(1)} async-done(((f32[4,128,1024]{2,1,0:T(8,128)}), f32[4,128,1024]{2,1,0:T(8,128)S(1)}, u32[]{:S(2)}, u32[]{:S(2)}) %all-to-all-start.1) | async-done | bytes 2097184 | tf_op jit(solution)/shard_map/all_to_all | solution.py:131
  312.8 1.1 gather_fusion.1
  313.9 0.6 gather.10
  314.6 1.3 multiply_reduce_fusion
  316.0 1.2 collective-permute-start
  317.3 8.4 %collective-permute-done = bf16[128,1024]{1,0:T(8,128)(2,1)S(1)} collective-permute-done((bf16[128,1024]{1,0:T(8,128)(2,1)S(1)}, bf16[128,1024]{1,0:T(8,128)(2,1)S(1)}, u32[]{:S(2)}, u32[]{:S(2)}) %collective-permute-start) | collective-permute-done | bytes 262176 | tf_op jit(solution)/shard_map/ppermute | solution.py:28
  326.1 3.8 %collective-permute-start.2 = (bf16[128,1024]{1,0:T(8,128)(2,1)S(1)}, bf16[128,1024]{1,0:T(8,128)(2,1)S(1)}, u32[]{:S(2)}, u32[]{:S(2)}) collective-permute-start(bf16[128,1024]{1,0:T(8,128)(2,1)S(1)} %add_convert_fusion.1), channel_id=1, source_target_pairs={{0,3},{1,0},{2,1},{3,2},{4,7},{5,4},{6,5},{7,6},{8,11},{9,8},{10,9... | collective-permute-start | bytes 786440 | tf_op jit(solution)/shard_map/ppermute | solution.py:32
  329.9 6.8 %collective-permute-done.1 = bf16[128,1024]{1,0:T(8,128)(2,1)S(1)} collective-permute-done((bf16[128,1024]{1,0:T(8,128)(2,1)S(1)}, bf16[128,1024]{1,0:T(8,128)(2,1)S(1)}, u32[]{:S(2)}, u32[]{:S(2)}) %collective-permute-start.1) | collective-permute-done | bytes 262176 | tf_op jit(solution)/shard_map/ppermute | solution.py:28
  336.8 1.9 collective-permute-done.2
  339.1 0.4 fusion.11
  339.6 2.1 fusion.40
  341.8 4.7 %convolution_bitcast_fusion = f32[16,8,8,128]{3,1,2,0:T(8,128)S(1)} fusion(bf16[4096,1024]{1,0:T(8,128)(2,1)} %all-gather.11.cloned.1.call-done, f32[4096]{0:T(1024)S(1)} %convert_element_type.80, f32[128]{0:T(128)S(1)} %add_rsqrt_fusion, f32[128]{0:T(128)S(1)} %broadcast_multiply_fusion.1, bf16[128,8192]{1,0:T(8,128)(2,1)S(1)} %constant_dynamic-update-slice_fusion, ...), kind=kOutput, calls=%fused_computation.27 | convolution fusion | flops 1076363264 | bytes 9978884 | tf_op jit(solution)/shard_map/dot_general | solution.py:143
  348.0 2.1 convolution_convert_fusion.1
  350.6 0.9 copy.46
  (77 shorter events, 5.5 us)
Async XLA Ops:
  8.0 33.1 %all-gather.5.cloned.1.call-start = ((), (), s32[]{:S(2)}) async-start(), calls=%async_computation.3 | async-start | bytes 1310720 | tf_op jit(solution)/shard_map/all_gather | solution.py:112
  8.7 263.5 %reduce-scatter.2.cloned.1.call-start = ((), (), s32[]{:S(2)}) async-start(), calls=%async_computation.4 | async-start | bytes 10485760 | tf_op jit(solution)/shard_map/reduce_scatter | solution.py:130
  41.1 3.2 copy-start
  101.1 1.9 copy-start.1
  129.0 210.6 %all-gather.9.cloned.1.call-start = ((), (), s32[]{:S(2)}) async-start(), calls=%async_computation.6 | async-start | bytes 2621440 | tf_op jit(solution)/shard_map/all_gather | solution.py:150
  129.5 212.2 %all-gather.11.cloned.1.call-start = ((), (), s32[]{:S(2)}) async-start(), calls=%async_computation.7 | async-start | bytes 10485760 | tf_op jit(solution)/shard_map/all_gather | solution.py:145
  272.2 4.3 %copy-start.5 = (s32[128,2]{0,1:T(2,128)S(1)}, s32[128,2]{0,1:T(2,128)}, u32[]{:S(2)}) copy-start(s32[128,2]{0,1:T(2,128)} %param.15) | copy-start | bytes 3076
  272.2 4.5 %copy-start.6 = (s32[1,4]{1,0:T(1,128)S(1)}, s32[1,4]{1,0:T(1,128)}, u32[]{:S(2)}) copy-start(s32[1,4]{1,0:T(1,128)} %param.16) | copy-start | bytes 52
  272.2 40.6 %all-to-all-start.1 = ((f32[4,128,1024]{2,1,0:T(8,128)}), f32[4,128,1024]{2,1,0:T(8,128)S(1)}, u32[]{:S(2)}, u32[]{:S(2)}) async-start(f32[4,128,1024]{2,1,0:T(8,128)} %bitcast.91), calls=%async_computation.2 | async-start | bytes 4194304 | tf_op jit(solution)/shard_map/all_to_all | solution.py:131
  275.9 72.1 %all-gather.7.cloned.1.call-start = ((), (), s32[]{:S(2)}) async-start(), calls=%async_computation.5 | async-start | bytes 2621440 | tf_op jit(solution)/shard_map/all_gather | solution.py:155
  313.9 2.0 copy-start.3
  313.9 11.8 %copy-start.4 = (bf16[4096]{0:T(1024)(128)(2,1)S(1)}, bf16[4096]{0:T(1024)(128)(2,1)}, u32[]{:S(2)}) copy-start(bf16[4096]{0:T(1024)(128)(2,1)} %param.20) | copy-start | bytes 24580
  316.0 22.8 %copy-start.2 = (bf16[128,1024]{1,0:T(8,128)(2,1)}, bf16[128,1024]{1,0:T(8,128)(2,1)S(1)}, u32[]{:S(2)}) copy-start(bf16[128,1024]{1,0:T(8,128)(2,1)S(1)} %add_convert_fusion.1) | copy-start | bytes 786436
  316.0 9.7 %collective-permute-start = (bf16[128,1024]{1,0:T(8,128)(2,1)S(1)}, bf16[128,1024]{1,0:T(8,128)(2,1)S(1)}, u32[]{:S(2)}, u32[]{:S(2)}) collective-permute-start(bf16[128,1024]{1,0:T(8,128)(2,1)S(1)} %add_convert_fusion.1), channel_id=1, source_target_pairs={{0,1},{1,2},{2,3},{3,0},{4,5},{5,6},{6,7},{7,4},{8,9},{9,10},{10,1... | collective-permute-start | bytes 786440 | tf_op jit(solution)/shard_map/ppermute | solution.py:28
  325.7 11.0 %collective-permute-start.1 = (bf16[128,1024]{1,0:T(8,128)(2,1)S(1)}, bf16[128,1024]{1,0:T(8,128)(2,1)S(1)}, u32[]{:S(2)}, u32[]{:S(2)}) collective-permute-start(bf16[128,1024]{1,0:T(8,128)(2,1)S(1)} %collective-permute-done), channel_id=1, source_target_pairs={{0,1},{1,2},{2,3},{3,0},{4,5},{5,6},{6,7},{7,4},{8,9},{9,10},{10,1... | collective-permute-start | bytes 786440 | tf_op jit(solution)/shard_map/ppermute | solution.py:28
  326.1 12.6 %collective-permute-start.2 = (bf16[128,1024]{1,0:T(8,128)(2,1)S(1)}, bf16[128,1024]{1,0:T(8,128)(2,1)S(1)}, u32[]{:S(2)}, u32[]{:S(2)}) collective-permute-start(bf16[128,1024]{1,0:T(8,128)(2,1)S(1)} %add_convert_fusion.1), channel_id=1, source_target_pairs={{0,3},{1,0},{2,1},{3,2},{4,7},{5,4},{6,5},{7,6},{8,11},{9,8},{10,9... | collective-permute-start | bytes 786440 | tf_op jit(solution)/shard_map/ppermute | solution.py:32
Sparse Core Ops, SparseCore 0:
  10.4 30.6 all-gather.4
  129.1 143.0 reduce-scatter.1
Sparse Core Ops, SparseCore 1:
  131.0 21.0 all-gather.8
  153.5 58.1 all-gather.10
  278.0 35.0 all-gather.6
